TPU v7x, 32 devices: a whole 2x2x4 slice. The times are simulated.
32 devices in a mesh: layer: 4 (over y, core), feat: 8 (over z, x).
Axes of the slice: x: 2, y: 2, z: 4, core: 2. Of those that a mesh axis runs over, the one named last changes fastest.
Arguments:
- acts: bfloat16 [4, 384, 2048], P('layer', 'feat'), may hold values from -64 to 64
- errors: bfloat16 [4, 384, 2048], P('layer', 'feat'), may hold values from -2.390625 to 2.390625
- enc_weight: bfloat16 [4, 2048, 8192], P('layer', None, 'feat'), may hold values from -0.0625 to 0.0625
- dec_weight: bfloat16 [4, 8192, 2048], P('layer', 'feat'), may hold values from -0.125 to 0.125
- chosen: int32 [384, 32], replicated, may hold values from 0 to 8191, all different within a row
Outputs:
- dec_grad: bfloat16 [4, 8192, 2048], P('layer', 'feat')
- enc_grad: bfloat16 [4, 2048, 8192], P('layer', None, 'feat')
Inputs may be any that keep to these rules, and one draw needn't show every extreme that they name: `chosen`: each row names 32 different features.
All inputs are finite; a program needn't handle non-finite values.
Results may differ from a plain program's by a relative error of at most 0.02.
Values may be sent and summed in bfloat16 or wider, within the bound.
No kernel may reach another device: no remote copies, remote signals or barrier semaphores. Data moves between devices by JAX's collectives and lax.ppermute only.
A program may use at most 64 MiB of HBM per device.

v0:
```python
import jax
import jax.numpy as jnp
from jax import lax
from jax.sharding import PartitionSpec as P


def slot_match(target, feat_dev):
    column_ids = jnp.arange(feat_dev, dtype=jnp.int32)
    return target[:, :, None] == column_ids[None, None, :]


def on_device(acts, errors, enc_weight, dec_weight, chosen):
    all_acts, all_errors = (
        lax.all_gather(acts, "feat", axis=1, tiled=True),
        lax.all_gather(errors, "feat", axis=1, tiled=True),
    )
    tokens = all_acts.shape[1]
    width = all_acts.shape[2]
    feat_dev = enc_weight.shape[2]
    first = lax.axis_index("feat") * feat_dev
    local_ids = chosen - first
    inside = (local_ids >= 0) & (local_ids < feat_dev)
    target = jnp.where(inside, local_ids, feat_dev)
    mask = jnp.any(slot_match(target, feat_dev), axis=1).astype(jnp.float32)
    squares = jnp.sum(jnp.square(all_acts.astype(jnp.float32)), axis=(1, 2))
    scale = 2.0 / (squares / (tokens * width) + 1e-06)
    partial_value = jnp.einsum(
        "ltd,ldf->tf", all_acts, enc_weight, preferred_element_type=jnp.float32
    )
    pre = lax.psum(partial_value.astype(jnp.bfloat16), "layer").astype(jnp.float32)
    codes = (pre * mask).astype(jnp.bfloat16)
    delta = (all_errors.astype(jnp.float32) * scale[:, None, None]).astype(jnp.bfloat16)
    dec_grad = jnp.einsum("tf,ltd->lfd", codes, delta, preferred_element_type=jnp.float32).astype(
        jnp.bfloat16
    )
    grad_partial = jnp.einsum("ltd,lfd->tf", delta, dec_weight, preferred_element_type=jnp.float32)
    code_grad = lax.psum(grad_partial.astype(jnp.bfloat16), "layer").astype(jnp.float32)
    pre_grad = (code_grad * mask).astype(jnp.bfloat16)
    enc_grad = jnp.einsum(
        "ltd,tf->ldf", all_acts, pre_grad, preferred_element_type=jnp.float32
    ).astype(jnp.bfloat16)
    return (dec_grad, enc_grad)


def solution(mesh):
    return jax.shard_map(
        on_device,
        mesh=mesh,
        in_specs=(
            P("layer", "feat", None),
            P("layer", "feat", None),
            P("layer", None, "feat"),
            P("layer", "feat", None),
            P(),
        ),
        out_specs=(P("layer", "feat", None), P("layer", None, "feat")),
        check_vma=False,
    )
```

profile of v0, /device:TPU:0, one launch (start us, length us, event | category | flops | bytes accessed | tf_op | source)
XLA Modules:
  0.0 178.2 jit_solution(6338268189235986830)
XLA Ops:
  7.2 0.0 all-gather.5.cloned.1.call-start
  7.2 0.7 all-gather.5.cloned.1.call-update
  7.9 0.0 all-gather.3.cloned.1.call-start
  7.9 0.7 all-gather.3.cloned.1.call-update
  8.6 0.0 all-reduce.3.cloned.1.call-start
  8.7 48.4 %all-gather.5.cloned.1.call-done = bf16[1,384,2048]{2,1,0:T(8,128)(2,1)} async-done(((bf16[1,48,2048]{2,1,0:T(8,128)(2,1)}), bf16[1,384,2048]{2,1,0:T(8,128)(2,1)}) %all-gather.5.cloned.1.call-update) | async-done | bytes 1572880 | tf_op jit(solution)/shard_map/all_gather | solution.py:14
  57.1 2.8 %multiply_reduce_fusion = f32[]{:T(128)} fusion(bf16[1,384,2048]{2,1,0:T(8,128)(2,1)} %all-gather.5.cloned.1.call-done), kind=kLoop, calls=%fused_computation.9 | loop fusion | flops 2359295 | bytes 1572868 | tf_op jit(solution)/shard_map/reduce_sum | solution.py:25
  60.6 5.3 %fusion.8 = bf16[384,1024]{1,0:T(8,128)(2,1)} fusion(bf16[1,2048,1024]{2,1,0:T(8,128)(2,1)} %param.7, bf16[1,384,2048]{2,1,0:T(8,128)(2,1)} %all-gather.5.cloned.1.call-done), kind=kOutput, calls=%fused_computation.15 | convolution fusion | flops 1611005952 | bytes 6553600 | tf_op jit(solution)/shard_map/ltd,ldf->tf/dot_general | solution.py:27
  65.9 0.0 copy-start.1
  65.9 35.9 %all-gather.3.cloned.1.call-done = bf16[1,384,2048]{2,1,0:T(8,128)(2,1)} async-done(((bf16[1,48,2048]{2,1,0:T(8,128)(2,1)}), bf16[1,384,2048]{2,1,0:T(8,128)(2,1)}) %all-gather.3.cloned.1.call-update) | async-done | bytes 1572880 | tf_op jit(solution)/shard_map/all_gather | solution.py:15
  101.9 0.0 copy-start.2
  101.9 5.5 %fusion.13 = bf16[384,1024]{1,0:T(8,128)(2,1)} fusion(bf16[1,1024,2048]{2,1,0:T(8,128)(2,1)} %param.8, bf16[1,384,2048]{2,1,0:T(8,128)(2,1)} %all-gather.3.cloned.1.call-done, f32[]{:T(128)S(6)} %div.8), kind=kOutput, calls=%fused_computation.16 | convolution fusion | flops 1613365248 | bytes 6553604 | tf_op jit(solution)/shard_map/ltd,lfd->tf/dot_general | solution.py:36
  107.3 0.0 all-reduce.3.cloned.1.call-update
  107.4 0.0 copy-done.1
  107.4 0.1 copy.10
  107.5 6.9 %fusion = pred[384,1024]{1,0:T(8,128)(4,1)S(1)} fusion(s32[384,32]{1,0:T(8,128)S(1)} %copy.10), kind=kLoop, calls=%fused_computation.1 | loop fusion | flops 24772608 | bytes 442368 | tf_op jit(solution)/shard_map/reduce_or | solution.py:24
  114.5 34.3 %all-reduce.3.cloned.1.call-done = (bf16[384,1024]{1,0:T(8,128)(2,1)}, bf16[384,1024]{1,0:T(8,128)(2,1)}) async-done(((bf16[384,1024]{1,0:T(8,128)(2,1)}, bf16[384,1024]{1,0:T(8,128)(2,1)}), (bf16[384,1024]{1,0:T(8,128)(2,1)}, bf16[384,1024]{1,0:T(8,128)(2,1)})) %all-reduce.3.cloned.1.call-update) | async-done | bytes 1572880 | tf_op jit(solution)/shard_map/psum | solution.py:30
  148.8 0.0 copy-done.2
  148.8 5.5 %convert_bitcast_fusion.1 = bf16[1,1024,2048]{1,2,0:T(8,128)(2,1)} fusion(bf16[1,384,2048]{2,1,0:T(8,128)(2,1)S(1)} %copy-done.2, f32[]{:T(128)S(6)} %div.8, pred[384,1024]{1,0:T(8,128)(4,1)S(1)} %fusion, bf16[384,1024]{1,0:T(8,128)(2,1)} %get-tuple-element.6), kind=kOutput, calls=%fused_computation.7 | convolution fusion | flops 1616248832 | bytes 6946820 | tf_op jit(solution)/shard_map/tf,ltd->lfd/dot_general | solution.py:33
  154.3 0.0 copy-start
  154.3 0.0 copy-start.3
  154.3 6.6 %copy.11 = bf16[1,1024,2048]{2,1,0:T(8,128)(2,1)} copy(bf16[1,1024,2048]{1,2,0:T(8,128)(2,1)} %convert_bitcast_fusion.1) | data formatting | bytes 8388608
  160.9 0.0 copy-done
  160.9 0.0 copy-done.3
  160.9 4.3 %convert_bitcast_fusion = bf16[1,2048,1024]{1,2,0:T(8,128)(2,1)} fusion(bf16[1,384,2048]{2,1,0:T(8,128)(2,1)S(1)} %copy-done, pred[384,1024]{1,0:T(8,128)(4,1)S(1)} %fusion, bf16[384,1024]{1,0:T(8,128)(2,1)S(1)} %copy-done.3), kind=kOutput, calls=%fused_computation.6 | convolution fusion | flops 1613889536 | bytes 6946816 | tf_op jit(solution)/shard_map/ltd,tf->ldf/dot_general | solution.py:39
  165.3 6.4 %copy.12 = bf16[1,2048,1024]{2,1,0:T(8,128)(2,1)} copy(bf16[1,2048,1024]{1,2,0:T(8,128)(2,1)} %convert_bitcast_fusion) | data formatting | bytes 8388608
  (1 shorter events, 0.0 us)
Async XLA Ops:
  7.2 49.9 %all-gather.5.cloned.1.call-start = ((), (), s32[]{:S(2)}) async-start(), calls=%async_computation.1 | async-start | bytes 1769472 | tf_op jit(solution)/shard_map/all_gather | solution.py:14
  7.9 94.0 %all-gather.3.cloned.1.call-start = ((), (), s32[]{:S(2)}) async-start(), calls=%async_computation | async-start | bytes 1769472 | tf_op jit(solution)/shard_map/all_gather | solution.py:15
  8.6 140.1 %all-reduce.3.cloned.1.call-start = ((), (), s32[]{:S(2)}) async-start(), calls=%async_computation.2 | async-start | bytes 3145728 | tf_op jit(solution)/shard_map/psum | solution.py:30
  65.9 41.4 %copy-start.1 = (s32[384,32]{0,1:T(8,128)S(1)}, s32[384,32]{0,1:T(8,128)}, u32[]{:S(2)}) copy-start(s32[384,32]{0,1:T(8,128)} %param.9) | copy-start | bytes 147460
  101.9 46.9 %copy-start.2 = (bf16[1,384,2048]{2,1,0:T(8,128)(2,1)S(1)}, bf16[1,384,2048]{2,1,0:T(8,128)(2,1)}, u32[]{:S(2)}) copy-start(bf16[1,384,2048]{2,1,0:T(8,128)(2,1)} %all-gather.3.cloned.1.call-done) | copy-start | bytes 4718596
  154.3 6.6 %copy-start = (bf16[1,384,2048]{2,1,0:T(8,128)(2,1)S(1)}, bf16[1,384,2048]{2,1,0:T(8,128)(2,1)}, u32[]{:S(2)}) copy-start(bf16[1,384,2048]{2,1,0:T(8,128)(2,1)} %all-gather.5.cloned.1.call-done) | copy-start | bytes 4718596
  154.3 6.6 %copy-start.3 = (bf16[384,1024]{1,0:T(8,128)(2,1)S(1)}, bf16[384,1024]{1,0:T(8,128)(2,1)}, u32[]{:S(2)}) copy-start(bf16[384,1024]{1,0:T(8,128)(2,1)} %get-tuple-element.7) | copy-start | bytes 2359300
Sparse Core Ops, SparseCore 0:
  10.2 46.8 all-gather.4
  59.3 42.5 all-gather.2
  107.5 41.2 all-reduce.2
where the time goes:
time: 179 us; the launch traced here: 178 us
  waiting for transfers between devices  120 us (67%)
  matrix products  20.7 us (12%)
  between operations  14.5 us (8%)
  local copies, waits for them, and re-layouts  13.1 us (7%)
  other arithmetic  9.77 us (5%)
    all_gather x1, waiting for transfers between devices, on_device(): lax.all_gather(acts, 'feat', axis=1, tiled=True)  48.4 us
    all_gather x1, waiting for transfers between devices, on_device(): lax.all_gather(errors, 'feat', axis=1, tiled=True)  35.9 us
    psum x1, waiting for transfers between devices, on_device(): lax.psum(partial_value.astype(jnp.bfloat16), 'layer').astype(jnp.float32)  34.3 us
    unnamed x10, local copies, waits for them, and re-layouts  13 us
    reduce_or x1, other arithmetic, on_device(): mask = jnp.any(slot_match(target, feat_dev), axis=1).astype(jnp.float32)  6.93 us
    dot_general x1, matrix products, on_device(): jnp.einsum('tf,ltd->lfd', codes, delta, preferred_element_type=jnp.float32)  5.55 us
    dot_general x1, matrix products, on_device(): jnp.einsum('ltd,lfd->tf', delta, dec_weight, preferred_element_type=jnp.f...  5.49 us
    dot_general x1, matrix products, on_device(): jnp.einsum('ltd,ldf->tf', all_acts, enc_weight, preferred_element_type=jn...  5.34 us
  transfers between devices with their start and end apart: 3, of which 3 were waited for; matrix products, arithmetic and copies ran while one was open for 9% of the time, Pallas kernels for 0%

commit v1 on v0

--- a/solution.py
+++ b/solution.py
@@ -27,7 +27,9 @@
     partial_value = jnp.einsum(
         "ltd,ldf->tf", all_acts, enc_weight, preferred_element_type=jnp.float32
     )
-    pre = lax.psum(partial_value.astype(jnp.bfloat16), "layer").astype(jnp.float32)
+    pre = jnp.sum(lax.all_gather(partial_value.astype(jnp.bfloat16), "layer"), axis=0).astype(
+        jnp.float32
+    )
     codes = (pre * mask).astype(jnp.bfloat16)
     delta = (all_errors.astype(jnp.float32) * scale[:, None, None]).astype(jnp.bfloat16)
     dec_grad = jnp.einsum("tf,ltd->lfd", codes, delta, preferred_element_type=jnp.float32).astype(

time: 179 us -> 191 us (1.067)
  waiting for transfers between devices: 120 us -> 130 us
  other arithmetic: 9.77 us -> 12.3 us
    all_gather x0 -> x1, waiting for transfers between devices: none -> 17.9 us  [on_device(): lax.all_gather(partial_value.astype(jnp.bfloat16), 'layer')]
    psum x1, waiting for transfers between devices: 34.3 us -> 21.5 us  [on_device(): lax.psum(grad_partial.astype(jnp.bfloat16), 'layer').astype(jnp.float32)]
    all_gather x1, waiting for transfers between devices: 35.9 us -> 41.2 us  [on_device(): lax.all_gather(errors, 'feat', axis=1, tiled=True)]
    reduce_sum x0 -> x1, other arithmetic: none -> 2.58 us  [on_device(): jnp.sum(lax.all_gather(partial_value.astype(jnp.bfloat16), 'layer'), axis=0)]
    unnamed x10 -> x8, local copies, waits for them, and re-layouts: 13 us -> 13 us
  transfers between devices with their start and end apart: 3 -> 4, of which waited for: 3 -> 4; matrix products, arithmetic and copies ran while one was open for 9% -> 14% of each run, Pallas kernels for 0% -> 0%
where the time goes in v1:
time: 191 us
  waiting for transfers between devices  130 us (68%)
  matrix products  20.1 us (11%)
  between operations  14.5 us (8%)
  local copies, waits for them, and re-layouts  13.1 us (7%)
  other arithmetic  12.3 us (6%)
    all_gather x1, waiting for transfers between devices, on_device(): lax.all_gather(acts, 'feat', axis=1, tiled=True)  48.4 us
    all_gather x1, waiting for transfers between devices, on_device(): lax.all_gather(errors, 'feat', axis=1, tiled=True)  41.2 us
    psum x1, waiting for transfers between devices, on_device(): lax.psum(grad_partial.astype(jnp.bfloat16), 'layer').astype(jnp.float32)  21.5 us
    all_gather x1, waiting for transfers between devices, on_device(): lax.all_gather(partial_value.astype(jnp.bfloat16), 'layer')  17.9 us
    unnamed x8, local copies, waits for them, and re-layouts  13 us
    reduce_or x1, other arithmetic, on_device(): mask = jnp.any(slot_match(target, feat_dev), axis=1).astype(jnp.float32)  6.93 us
    dot_general x1, matrix products, on_device(): jnp.einsum('ltd,tf->ldf', all_acts, pre_grad, preferred_element_type=jnp....  5.54 us
    dot_general x1, matrix products, on_device(): jnp.einsum('ltd,lfd->tf', delta, dec_weight, preferred_element_type=jnp.f...  5.37 us
  transfers between devices with their start and end apart: 4, of which 4 were waited for; matrix products, arithmetic and copies ran while one was open for 14% of the time, Pallas kernels for 0%

profile of v1, /device:TPU:0, one launch (start us, length us, event | category | flops | bytes accessed | tf_op | source)
XLA Modules:
  0.0 190.7 jit_solution(6892999027449176999)
XLA Ops:
  7.2 0.0 all-gather.7.cloned.1.call-start
  7.2 0.7 all-gather.7.cloned.1.call-update
  7.9 0.0 all-gather.5.cloned.1.call-start
  7.9 0.7 all-gather.5.cloned.1.call-update
  8.6 0.0 all-reduce.2.cloned.1.call-start
  8.7 48.4 %all-gather.7.cloned.1.call-done = bf16[1,384,2048]{2,1,0:T(8,128)(2,1)} async-done(((bf16[1,48,2048]{2,1,0:T(8,128)(2,1)}), bf16[1,384,2048]{2,1,0:T(8,128)(2,1)}) %all-gather.7.cloned.1.call-update) | async-done | bytes 1572880 | tf_op jit(solution)/shard_map/all_gather | solution.py:14
  57.1 2.8 %multiply_reduce_fusion = f32[]{:T(128)} fusion(bf16[1,384,2048]{2,1,0:T(8,128)(2,1)} %all-gather.7.cloned.1.call-done), kind=kLoop, calls=%fused_computation.9 | loop fusion | flops 2359295 | bytes 1572868 | tf_op jit(solution)/shard_map/reduce_sum | solution.py:25
  60.6 0.0 copy-start
  60.6 41.2 %all-gather.5.cloned.1.call-done = bf16[1,384,2048]{2,1,0:T(8,128)(2,1)} async-done(((bf16[1,48,2048]{2,1,0:T(8,128)(2,1)}), bf16[1,384,2048]{2,1,0:T(8,128)(2,1)}) %all-gather.5.cloned.1.call-update) | async-done | bytes 1572880 | tf_op jit(solution)/shard_map/all_gather | solution.py:15
  101.8 5.4 %fusion.13 = bf16[384,1024]{1,0:T(8,128)(2,1)} fusion(bf16[1,1024,2048]{2,1,0:T(8,128)(2,1)} %param.8, bf16[1,384,2048]{2,1,0:T(8,128)(2,1)} %all-gather.5.cloned.1.call-done, f32[]{:T(128)S(6)} %div.8), kind=kOutput, calls=%fused_computation.16 | convolution fusion | flops 1613365248 | bytes 6553604 | tf_op jit(solution)/shard_map/ltd,lfd->tf/dot_general | solution.py:38
  107.2 0.0 all-reduce.2.cloned.1.call-update
  107.2 0.0 copy-start.1
  107.3 0.0 all-gather.9.cloned.1.call-start
  107.3 0.0 copy-done
  107.3 4.9 %fusion.8 = bf16[384,1024]{1,0:T(8,128)(2,1)} fusion(bf16[1,2048,1024]{2,1,0:T(8,128)(2,1)} %param.7, bf16[1,384,2048]{2,1,0:T(8,128)(2,1)S(1)} %copy-done), kind=kOutput, calls=%fused_computation.15 | convolution fusion | flops 1611005952 | bytes 6553600 | tf_op jit(solution)/shard_map/ltd,ldf->tf/dot_general | solution.py:27
  112.2 0.0 all-gather.9.cloned.1.call-update
  112.2 0.0 copy-done.1
  112.2 0.1 copy.10
  112.4 6.9 %fusion = pred[384,1024]{1,0:T(8,128)(4,1)S(1)} fusion(s32[384,32]{1,0:T(8,128)S(1)} %copy.10), kind=kLoop, calls=%fused_computation.1 | loop fusion | flops 24772608 | bytes 442368 | tf_op jit(solution)/shard_map/reduce_or | solution.py:24
  119.3 21.5 %all-reduce.2.cloned.1.call-done = bf16[384,1024]{1,0:T(8,128)(2,1)} async-done(((bf16[384,1024]{1,0:T(8,128)(2,1)}), bf16[384,1024]{1,0:T(8,128)(2,1)}) %all-reduce.2.cloned.1.call-update) | async-done | bytes 786448 | tf_op jit(solution)/shard_map/psum | solution.py:39
  140.8 5.5 %convert_bitcast_fusion = bf16[1,2048,1024]{1,2,0:T(8,128)(2,1)} fusion(bf16[1,384,2048]{2,1,0:T(8,128)(2,1)S(1)} %copy-done, pred[384,1024]{1,0:T(8,128)(4,1)S(1)} %fusion, bf16[384,1024]{1,0:T(8,128)(2,1)} %all-reduce.2.cloned.1.call-done), kind=kOutput, calls=%fused_computation.6 | convolution fusion | flops 1613889536 | bytes 6946816 | tf_op jit(solution)/shard_map/ltd,tf->ldf/dot_general | solution.py:41
  146.3 6.5 %copy.12 = bf16[1,2048,1024]{2,1,0:T(8,128)(2,1)} copy(bf16[1,2048,1024]{1,2,0:T(8,128)(2,1)} %convert_bitcast_fusion) | data formatting | bytes 8388608
  152.9 0.0 copy-start.2
  152.9 17.9 %all-gather.9.cloned.1.call-done = bf16[1536,1024]{1,0:T(8,128)(2,1)} async-done(((bf16[384,1024]{1,0:T(8,128)(2,1)}), bf16[1536,1024]{1,0:T(8,128)(2,1)}) %all-gather.9.cloned.1.call-update) | async-done | bytes 3145744 | tf_op jit(solution)/shard_map/all_gather | solution.py:30
  170.8 2.6 %reduce_sum.22 = bf16[384,1024]{1,0:T(8,128)(2,1)S(1)} reduce(bf16[4,384,1024]{2,1,0:T(8,128)(2,1)} %bitcast.30, bf16[]{:T(256)} %constant.26.clone.1), dimensions={0}, to_apply=%region_2.3 | reduce | flops 1179648 | bytes 3932162 | tf_op jit(solution)/shard_map/reduce_sum | solution.py:30
  173.3 0.0 copy-done.2
  173.3 4.3 %convert_bitcast_fusion.1 = bf16[1,1024,2048]{1,2,0:T(8,128)(2,1)} fusion(bf16[1,384,2048]{2,1,0:T(8,128)(2,1)S(1)} %copy-done.2, f32[]{:T(128)S(6)} %div.8, pred[384,1024]{1,0:T(8,128)(4,1)S(1)} %fusion, bf16[384,1024]{1,0:T(8,128)(2,1)S(1)} %reduce_sum.22), kind=kOutput, calls=%fused_computation.7 | convolution fusion | flops 1616248832 | bytes 6946820 | tf_op jit(solution)/shard_map/tf,ltd->lfd/dot_general | solution.py:35
  177.7 6.4 %copy.11 = bf16[1,1024,2048]{2,1,0:T(8,128)(2,1)} copy(bf16[1,1024,2048]{1,2,0:T(8,128)(2,1)} %convert_bitcast_fusion.1) | data formatting | bytes 8388608
  (1 shorter events, 0.0 us)
Async XLA Ops:
  7.2 49.9 %all-gather.7.cloned.1.call-start = ((), (), s32[]{:S(2)}) async-start(), calls=%async_computation.1 | async-start | bytes 1769472 | tf_op jit(solution)/shard_map/all_gather | solution.py:14
  7.9 93.9 %all-gather.5.cloned.1.call-start = ((), (), s32[]{:S(2)}) async-start(), calls=%async_computation | async-start | bytes 1769472 | tf_op jit(solution)/shard_map/all_gather | solution.py:15
  8.6 132.1 %all-reduce.2.cloned.1.call-start = ((), (), s32[]{:S(2)}) async-start(), calls=%async_computation.2 | async-start | bytes 1572864 | tf_op jit(solution)/shard_map/psum | solution.py:39
  60.6 46.7 %copy-start = (bf16[1,384,2048]{2,1,0:T(8,128)(2,1)S(1)}, bf16[1,384,2048]{2,1,0:T(8,128)(2,1)}, u32[]{:S(2)}) copy-start(bf16[1,384,2048]{2,1,0:T(8,128)(2,1)} %all-gather.7.cloned.1.call-done) | copy-start | bytes 4718596
  107.2 5.0 %copy-start.1 = (s32[384,32]{0,1:T(8,128)S(1)}, s32[384,32]{0,1:T(8,128)}, u32[]{:S(2)}) copy-start(s32[384,32]{0,1:T(8,128)} %param.9) | copy-start | bytes 147460
  107.3 63.5 %all-gather.9.cloned.1.call-start = ((), (), s32[]{:S(2)}) async-start(), calls=%async_computation.3 | async-start | bytes 3932160 | tf_op jit(solution)/shard_map/all_gather | solution.py:30
  152.9 20.5 %copy-start.2 = (bf16[1,384,2048]{2,1,0:T(8,128)(2,1)S(1)}, bf16[1,384,2048]{2,1,0:T(8,128)(2,1)}, u32[]{:S(2)}) copy-start(bf16[1,384,2048]{2,1,0:T(8,128)(2,1)} %all-gather.5.cloned.1.call-done) | copy-start | bytes 4718596
Sparse Core Ops, SparseCore 0:
  10.2 46.8 all-gather.6
  59.3 42.5 all-gather.4
  107.4 33.3 all-reduce.1
  142.2 28.4 all-gather.8
